TPU v7x, 32 devices: a whole 2x2x4 slice. The times are simulated.
32 devices in a mesh: rep: 2 (over core), grp: 16 (over z, y, x).
Axes of the slice: x: 2, y: 2, z: 4, core: 2. Of those that a mesh axis runs over, the one named last changes fastest.
Arguments:
- grad_parts: float32 [2, 1024, 9216], P('rep', 'grp'), may hold values from -6 to 6
- gain_grad_parts: float32 [2, 2, 1024], P('rep', None, 'grp'), may hold values from -6 to 6
- weights: float32 [1024, 9216], P('grp'), may hold values from -0.1875 to 0.1875
- basis: float32 [1024, 256], P('grp'), may hold values from -0.1875 to 0.1875
- moment_first: float32 [9216, 256], P('grp'), may hold values from -12 to 12
- moment_second: float32 [9216, 256], P('grp'), may hold values from 0.01 to 1
- gains: float32 [2, 1024], P(None, 'grp'), may hold values from 0.5 to 1.5
- gain_first: float32 [2, 1024], P(None, 'grp'), may hold values from -12 to 12
- gain_second: float32 [2, 1024], P(None, 'grp'), may hold values from 0.01 to 1
Outputs:
- new_weights: float32 [1024, 9216], P('grp')
- new_first: float32 [9216, 256], P('grp')
- new_second: float32 [9216, 256], P('grp')
- new_basis: float32 [1024, 256], P('grp')
- new_gains: float32 [2, 1024], P(None, 'grp')
- new_gain_first: float32 [2, 1024], P(None, 'grp')
- new_gain_second: float32 [2, 1024], P(None, 'grp')
All inputs are finite; a program needn't handle non-finite values.
Results may differ from a plain program's by a relative error of at most 0.0001.
Values sent between devices are 32-bit elements; how exact they have to be, the bound alone decides.
A program may use at most 64 MiB of HBM per device.

v0:
```python
import jax
import jax.numpy as jnp
from jax import lax
from jax.sharding import PartitionSpec as P

NS_STEPS = 3
beta_first = 0.9
beta_second = 0.999
learn_rate = 0.1
galore_scale = 0.25
adam_eps = 1e-08


def exact_dot(left, right):
    return jnp.dot(left, right, precision=lax.Precision.HIGHEST, preferred_element_type=jnp.float32)


def body(
    grad_parts,
    gain_grad_parts,
    weights,
    basis,
    moment_first,
    moment_second,
    gains,
    gain_first,
    gain_second,
):
    corr_first = 1.0 - beta_first**10
    corr_second = 1.0 - beta_second**10
    local_grad = grad_parts[0]
    local_gain = gain_grad_parts[0]
    source, gain_grad = lax.psum((local_grad, local_gain), "rep")
    col_block = lax.all_to_all(source, "grp", split_axis=1, concat_axis=0, tiled=True)
    full_basis = lax.all_gather(basis, "grp", axis=0, tiled=True)
    projected = exact_dot(col_block.T, full_basis)
    new_first = beta_first * moment_first + (1.0 - beta_first) * projected
    new_second = beta_second * moment_second + (1.0 - beta_second) * projected * projected
    direction = new_first / corr_first / (jnp.sqrt(new_second / corr_second) + adam_eps)
    subspace = lax.psum_scatter(
        exact_dot(col_block, projected), "grp", scatter_dimension=0, tiled=True
    )
    update_cols = exact_dot(full_basis, direction.T)
    update = lax.all_to_all(update_cols, "grp", split_axis=0, concat_axis=1, tiled=True)
    new_weights = weights - learn_rate * galore_scale * update
    gram = lax.psum(exact_dot(subspace.T, subspace), "grp")
    scale = jnp.sqrt(jnp.sqrt(jnp.sum(gram * gram) + 1e-06))
    iterate = subspace / scale
    current = lax.psum(exact_dot(iterate.T, iterate), "grp")
    for step in range(NS_STEPS):
        iterate = 1.5 * iterate - 0.5 * exact_dot(iterate, current)
        if step + 1 < NS_STEPS:
            current = lax.psum(exact_dot(iterate.T, iterate), "grp")
    new_gain_first = beta_first * gain_first + (1.0 - beta_first) * gain_grad
    new_gain_second = beta_second * gain_second + (1.0 - beta_second) * gain_grad * gain_grad
    new_gains = gains - learn_rate * (new_gain_first / corr_first) / (
        jnp.sqrt(new_gain_second / corr_second) + adam_eps
    )
    return (new_weights, new_first, new_second, iterate, new_gains, new_gain_first, new_gain_second)


def solution(mesh):
    in_specs = (
        P("rep", "grp", None),
        P("rep", None, "grp"),
        P("grp", None),
        P("grp", None),
        P("grp", None),
        P("grp", None),
        P(None, "grp"),
        P(None, "grp"),
        P(None, "grp"),
    )
    out_specs = (
        P("grp", None),
        P("grp", None),
        P("grp", None),
        P("grp", None),
        P(None, "grp"),
        P(None, "grp"),
        P(None, "grp"),
    )
    return jax.shard_map(body, mesh=mesh, in_specs=in_specs, out_specs=out_specs, check_vma=False)
```

profile of v0, /device:TPU:0, one launch (start us, length us, event | category | flops | bytes accessed | tf_op | source)
XLA Modules:
  0.0 698.1 jit_solution(16123633923945637209)
XLA Ops:
  8.0 0.0 all-reduce.6.cloned.1.call-start
  8.0 2.2 all_to_all.24
  10.2 2.3 copy.34
  12.5 0.0 all-reduce.6.cloned.1.call-update
  12.6 25.1 %all-reduce.6.cloned.1.call-done = f32[64,16,576]{2,0,1:T(8,128)} async-done(((f32[64,16,576]{2,0,1:T(8,128)}), f32[64,16,576]{2,0,1:T(8,128)}) %all-reduce.6.cloned.1.call-update) | async-done | bytes 2359312 | tf_op jit(solution)/shard_map/psum | solution.py:33
  37.7 6.8 all-to-all-start
  44.5 0.0 all-gather.2.cloned.1.call-start
  44.6 0.5 all-gather.2.cloned.1.call-update
  45.1 0.0 reduce-scatter.4.cloned.1.call-start
  45.1 83.0 %all-gather.2.cloned.1.call-done = f32[1024,256]{1,0:T(8,128)} async-done(((f32[64,256]{1,0:T(8,128)}), f32[1024,256]{1,0:T(8,128)}) %all-gather.2.cloned.1.call-update) | async-done | bytes 1048592 | tf_op jit(solution)/shard_map/all_gather | solution.py:35
  128.1 0.0 all-to-all-done
  128.1 6.7 multiply_add_fusion
  134.8 0.0 copy-start
  134.8 5.5 convolution_bitcast_fusion.1
  140.3 2.6 copy.38
  142.9 0.0 reduce-scatter.4.cloned.1.call-update
  142.9 0.0 copy-done
  142.9 3.8 convolution_bitcast_fusion
  146.7 2.1 copy.35
  148.8 4.5 all-to-all-start.1
  153.3 0.0 copy-start.4
  153.3 0.0 copy-start.1
  153.3 0.0 copy-start.2
  153.3 0.0 copy-start.3
  153.3 0.0 all-reduce.8.cloned.1.call-start
  153.4 80.3 %reduce-scatter.4.cloned.1.call-done = f32[64,256]{1,0:T(8,128)} async-done(((f32[1024,256]{1,0:T(8,128)}), f32[64,256]{1,0:T(8,128)}) %reduce-scatter.4.cloned.1.call-update) | async-done | bytes 65552
  233.7 2.0 fusion.18
  235.8 0.0 all-reduce.8.cloned.1.call-update
  235.8 0.2 all-reduce.10.cloned.1.call-start
  236.0 109.0 %all-reduce.8.cloned.1.call-done = f32[256,256]{1,0:T(8,128)} async-done(((f32[256,256]{1,0:T(8,128)}), f32[256,256]{1,0:T(8,128)}) %all-reduce.8.cloned.1.call-update) | async-done | bytes 262160 | tf_op jit(solution)/shard_map/psum | solution.py:46
  345.0 1.6 multiply_reduce_fusion
  347.4 2.0 fusion.12
  349.4 0.0 all-reduce.10.cloned.1.call-update
  349.5 0.0 all-reduce.12.cloned.1.call-start
  349.5 107.5 %all-reduce.10.cloned.1.call-done = f32[256,256]{1,0:T(8,128)} async-done(((f32[256,256]{1,0:T(8,128)}), f32[256,256]{1,0:T(8,128)}) %all-reduce.10.cloned.1.call-update) | async-done | bytes 262160 | tf_op jit(solution)/shard_map/psum | solution.py:49
  457.0 1.2 fusion.2
  458.2 1.1 fusion.19
  459.3 0.0 all-reduce.12.cloned.1.call-update
  459.4 0.0 all-reduce.14.cloned.1.call-start
  459.4 109.6 %all-reduce.12.cloned.1.call-done = f32[256,256]{1,0:T(8,128)} async-done(((f32[256,256]{1,0:T(8,128)}), f32[256,256]{1,0:T(8,128)}) %all-reduce.12.cloned.1.call-update) | async-done | bytes 262160 | tf_op jit(solution)/shard_map/psum | solution.py:53
  569.0 1.2 fusion.1
  570.2 1.1 fusion.20
  571.3 0.0 all-reduce.14.cloned.1.call-update
  571.3 0.0 copy-done.4
  571.4 2.5 psum.47
  573.8 0.0 copy-done.1
  573.8 0.0 copy-done.2
  573.8 0.0 copy-done.3
  573.8 0.6 divide_subtract_fusion
  574.4 106.6 %all-reduce.14.cloned.1.call-done = f32[256,256]{1,0:T(8,128)} async-done(((f32[256,256]{1,0:T(8,128)}), f32[256,256]{1,0:T(8,128)}) %all-reduce.14.cloned.1.call-update) | async-done | bytes 262160 | tf_op jit(solution)/shard_map/psum | solution.py:53
  681.0 1.8 fusion
  682.8 0.0 all-to-all-done.1
  682.8 0.2 multiply_bitcast_fusion
  683.1 1.5 copy.36
  684.6 2.0 mul.101
  686.6 4.0 sub.15
Async XLA Ops:
  8.0 29.7 %all-reduce.6.cloned.1.call-start = ((), (), s32[]{:S(2)}) async-start(), calls=%async_computation.3 | async-start | bytes 5242880 | tf_op jit(solution)/shard_map/psum | solution.py:33
  37.7 90.4 %all-to-all-start = ((f32[64,16,576]{2,0,1:T(8,128)}), f32[64,16,576]{2,0,1:T(8,128)S(1)}, u32[]{:S(2)}, u32[]{:S(2)}) async-start(f32[64,16,576]{2,0,1:T(8,128)} %all-reduce.6.cloned.1.call-done), calls=%async_computation | async-start | bytes 5242880 | tf_op jit(solution)/shard_map/all_to_all | solution.py:34
  44.5 83.6 %all-gather.2.cloned.1.call-start = ((), (), s32[]{:S(2)}) async-start(), calls=%async_computation.4 | async-start | bytes 1114112 | tf_op jit(solution)/shard_map/all_gather | solution.py:35
  45.1 188.7 %reduce-scatter.4.cloned.1.call-start = ((), (), s32[]{:S(2)}) async-start(), calls=%async_computation.9 | async-start | bytes 1114112
  134.8 8.1 %copy-start = (f32[576,256]{1,0:T(8,128)}, f32[576,256]{1,0:T(8,128)S(1)}, u32[]{:S(2)}) copy-start(f32[576,256]{1,0:T(8,128)S(1)} %get-tuple-element.31) | copy-start | bytes 1769476
  148.8 534.0 %all-to-all-start.1 = ((f32[16,64,576]{2,1,0:T(8,128)}), f32[16,64,576]{2,1,0:T(8,128)S(1)}, u32[]{:S(2)}, u32[]{:S(2)}) async-start(f32[16,64,576]{2,1,0:T(8,128)} %bitcast.30), calls=%async_computation.1 | async-start | bytes 5242880 | tf_op jit(solution)/shard_map/all_to_all | solution.py:44
  153.3 418.1 %copy-start.4 = (f32[1,2,64]{2,1,0:T(2,128)S(1)}, f32[1,2,64]{2,1,0:T(2,128)}, u32[]{:S(2)}) copy-start(f32[1,2,64]{2,1,0:T(2,128)} %param.10) | copy-start | bytes 1540
  153.3 420.5 %copy-start.1 = (f32[2,64]{1,0:T(2,128)S(1)}, f32[2,64]{1,0:T(2,128)}, u32[]{:S(2)}) copy-start(f32[2,64]{1,0:T(2,128)} %param.15) | copy-start | bytes 1540
  153.3 420.5 %copy-start.2 = (f32[2,64]{1,0:T(2,128)S(1)}, f32[2,64]{1,0:T(2,128)}, u32[]{:S(2)}) copy-start(f32[2,64]{1,0:T(2,128)} %param.16) | copy-start | bytes 1540
  153.3 420.5 %copy-start.3 = (f32[2,64]{1,0:T(2,128)S(1)}, f32[2,64]{1,0:T(2,128)}, u32[]{:S(2)}) copy-start(f32[2,64]{1,0:T(2,128)} %param.17) | copy-start | bytes 1540
  153.3 191.7 %all-reduce.8.cloned.1.call-start = ((), (), s32[]{:S(2)}) async-start(), calls=%async_computation.5 | async-start | bytes 524288 | tf_op jit(solution)/shard_map/psum | solution.py:46
  235.8 221.2 %all-reduce.10.cloned.1.call-start = ((), (), s32[]{:S(2)}) async-start(), calls=%async_computation.6 | async-start | bytes 524288 | tf_op jit(solution)/shard_map/psum | solution.py:49
  349.5 219.5 %all-reduce.12.cloned.1.call-start = ((), (), s32[]{:S(2)}) async-start(), calls=%async_computation.7 | async-start | bytes 524288 | tf_op jit(solution)/shard_map/psum | solution.py:53
  459.4 221.6 %all-reduce.14.cloned.1.call-start = ((), (), s32[]{:S(2)}) async-start(), calls=%async_computation.8 | async-start | bytes 524288 | tf_op jit(solution)/shard_map/psum | solution.py:53
Sparse Core Ops, SparseCore 0:
  12.7 24.9 all-reduce.5
Sparse Core Ops, SparseCore 1:
  47.8 80.3 all-gather.1
  143.0 90.7 reduce-scatter.3
  239.4 105.6 all-reduce.7
  350.9 106.1 all-reduce.9
  462.8 106.1 all-reduce.11
  574.8 106.1 all-reduce.13
where the time goes:
time: 699 us; the launch traced here: 698 us
  waiting for transfers between devices  622 us (89%)
  matrix products  26.5 us (4%)
  between operations  16.4 us (2%)
  local copies, waits for them, and re-layouts  12.7 us (2%)
  starting transfers between devices  11.8 us (2%)
    psum x3, waiting for transfers between devices, body(): current = lax.psum(exact_dot(iterate.T, iterate), 'grp')  324 us
    psum x1, waiting for transfers between devices, body(): gram = lax.psum(exact_dot(subspace.T, subspace), 'grp')  109 us
    all_gather x1, waiting for transfers between devices, body(): full_basis = lax.all_gather(basis, 'grp', axis=0, tiled=True)  83 us
    unnamed x8, waiting for transfers between devices  81 us
    dot_general x10, matrix products, exact_dot(): jnp.dot(left, right, precision=lax.Precision.HIGHEST, preferred_element_t...  26.5 us
    psum x1, waiting for transfers between devices, body(): source, gain_grad = lax.psum((local_grad, local_gain), 'rep')  25.1 us
  transfers between devices with their start and end apart: 9, of which 7 were waited for; matrix products, arithmetic and copies ran while one was open for 3% of the time, Pallas kernels for 0%

commit v1 on v0

--- a/solution.py
+++ b/solution.py
@@ -43,7 +43,7 @@
     update_cols = exact_dot(full_basis, direction.T)
     update = lax.all_to_all(update_cols, "grp", split_axis=0, concat_axis=1, tiled=True)
     new_weights = weights - learn_rate * galore_scale * update
-    gram = lax.psum(exact_dot(subspace.T, subspace), "grp")
+    gram = jnp.sum(lax.all_gather(exact_dot(subspace.T, subspace), "grp"), axis=0)
     scale = jnp.sqrt(jnp.sqrt(jnp.sum(gram * gram) + 1e-06))
     iterate = subspace / scale
     current = lax.psum(exact_dot(iterate.T, iterate), "grp")

time: 699 us -> 669 us (0.957)
  waiting for transfers between devices: 622 us -> 592 us
    psum x1 -> x0, waiting for transfers between devices: 109 us -> none  [body(): gram = lax.psum(exact_dot(subspace.T, subspace), 'grp')]
    all_gather x0 -> x1, waiting for transfers between devices: none -> 90.9 us  [body(): lax.all_gather(exact_dot(subspace.T, subspace), 'grp')]
    psum x3, waiting for transfers between devices: 324 us -> 315 us  [body(): current = lax.psum(exact_dot(iterate.T, iterate), 'grp')]
where the time goes in v1:
time: 669 us; the launch traced here: 668 us
  waiting for transfers between devices  592 us (88%)
  matrix products  25.4 us (4%)
  between operations  16.4 us (2%)
  local copies, waits for them, and re-layouts  12.8 us (2%)
  starting transfers between devices  11 us (2%)
  other arithmetic  8.02 us (1%)
    psum x3, waiting for transfers between devices, body(): current = lax.psum(exact_dot(iterate.T, iterate), 'grp')  315 us
    all_gather x1, waiting for transfers between devices, body(): lax.all_gather(exact_dot(subspace.T, subspace), 'grp')  90.9 us
    all_gather x1, waiting for transfers between devices, body(): full_basis = lax.all_gather(basis, 'grp', axis=0, tiled=True)  83 us
    unnamed x8, waiting for transfers between devices  78.2 us
    dot_general x10, matrix products, exact_dot(): jnp.dot(left, right, precision=lax.Precision.HIGHEST, preferred_element_t...  25.4 us
    psum x1, waiting for transfers between devices, body(): source, gain_grad = lax.psum((local_grad, local_gain), 'rep')  25.1 us
  transfers between devices with their start and end apart: 9, of which 7 were waited for; matrix products, arithmetic and copies ran while one was open for 3% of the time, Pallas kernels for 0%

profile of v1, /device:TPU:0, one launch (start us, length us, event | category | flops | bytes accessed | tf_op | source)
XLA Modules:
  0.0 668.0 jit_solution(6917661218397143144)
XLA Ops:
  8.0 0.0 all-reduce.5.cloned.1.call-start
  8.0 2.2 all_to_all.24
  10.2 2.3 copy.38
  12.5 0.0 all-reduce.5.cloned.1.call-update
  12.6 0.0 copy-start.1
  12.6 25.1 %all-reduce.5.cloned.1.call-done = f32[64,16,576]{2,0,1:T(8,128)} async-done(((f32[64,16,576]{2,0,1:T(8,128)}), f32[64,16,576]{2,0,1:T(8,128)}) %all-reduce.5.cloned.1.call-update) | async-done | bytes 2359312 | tf_op jit(solution)/shard_map/psum | solution.py:33
  37.7 6.8 %all-to-all-start = ((f32[64,16,576]{2,0,1:T(8,128)}), f32[64,16,576]{2,0,1:T(8,128)S(1)}, u32[]{:S(2)}, u32[]{:S(2)}) async-start(f32[64,16,576]{2,0,1:T(8,128)} %all-reduce.5.cloned.1.call-done), calls=%async_computation | async-start | bytes 5242880 | tf_op jit(solution)/shard_map/all_to_all | solution.py:34
  44.5 0.0 all-gather.4.cloned.1.call-start
  44.6 0.5 all-gather.4.cloned.1.call-update
  45.1 0.0 reduce-scatter.4.cloned.1.call-start
  45.1 83.0 %all-gather.4.cloned.1.call-done = f32[1024,256]{1,0:T(8,128)} async-done(((f32[64,256]{1,0:T(8,128)}), f32[1024,256]{1,0:T(8,128)}) %all-gather.4.cloned.1.call-update) | async-done | bytes 1048592 | tf_op jit(solution)/shard_map/all_gather | solution.py:35
  128.1 0.0 all-to-all-done
  128.1 0.0 copy-done.1
  128.1 6.7 %multiply_add_fusion = (f32[576,256]{1,0:T(8,128)}, f32[576,256]{1,0:T(8,128)}, f32[576,256]{1,0:T(8,128)S(1)}) fusion(f32[576,256]{1,0:T(8,128)S(1)} %copy-done.1, f32[576,256]{1,0:T(8,128)} %param.14, f32[1024,576]{1,0:T(8,128)S(1)} %bitcast.29, f32[1024,256]{1,0:T(8,128)} %all-gather.4.cloned.1.call-done), kind=kOutput, calls=%fused_computation.16 | convolution fusion | flops 1812971520 | bytes 6356992 | tf_op jit(solution)/shard_map/dot_general | solution.py:15
  134.8 5.5 convolution_bitcast_fusion.1
  140.4 0.0 copy-start
  140.4 2.6 copy.42
  143.0 0.0 reduce-scatter.4.cloned.1.call-update
  143.0 0.2 all-gather.6.cloned.1.call-start
  143.2 77.6 %reduce-scatter.4.cloned.1.call-done = f32[64,256]{1,0:T(8,128)} async-done(((f32[1024,256]{1,0:T(8,128)}), f32[64,256]{1,0:T(8,128)}) %reduce-scatter.4.cloned.1.call-update) | async-done | bytes 65552
  220.8 2.0 fusion.18
  222.8 0.0 all-gather.6.cloned.1.call-update
  222.9 0.0 copy-done
  222.9 3.6 convolution_bitcast_fusion
  226.5 2.1 copy.39
  228.6 3.7 all-to-all-start.1
  232.3 0.0 copy-start.2
  232.3 0.0 all-reduce.7.cloned.1.call-start
  232.4 90.9 %all-gather.6.cloned.1.call-done = f32[4096,256]{1,0:T(8,128)} async-done(((f32[256,256]{1,0:T(8,128)}), f32[4096,256]{1,0:T(8,128)}) %all-gather.6.cloned.1.call-update) | async-done | bytes 4194320 | tf_op jit(solution)/shard_map/all_gather | solution.py:46
  323.3 0.0 copy-start.6
  323.3 0.0 copy-start.3
  323.3 0.0 copy-start.4
  323.3 0.0 copy-start.5
  323.3 2.5 reduce_sum.18
  325.8 0.7 multiply_reduce_fusion
  327.2 0.0 copy-done.2
  327.2 1.1 fusion.12
  328.4 0.0 all-reduce.7.cloned.1.call-update
  328.4 0.0 all-reduce.9.cloned.1.call-start
  328.5 106.9 %all-reduce.7.cloned.1.call-done = f32[256,256]{1,0:T(8,128)} async-done(((f32[256,256]{1,0:T(8,128)}), f32[256,256]{1,0:T(8,128)}) %all-reduce.7.cloned.1.call-update) | async-done | bytes 262160 | tf_op jit(solution)/shard_map/psum | solution.py:49
  435.3 1.2 fusion.2
  436.5 1.1 fusion.19
  437.6 0.0 all-reduce.9.cloned.1.call-update
  437.7 0.0 all-reduce.11.cloned.1.call-start
  437.7 0.0 copy-done.6
  437.7 2.5 psum.39
  440.2 0.0 copy-done.3
  440.2 0.0 copy-done.4
  440.2 0.0 copy-done.5
  440.2 0.6 divide_subtract_fusion
  440.8 106.5 %all-reduce.9.cloned.1.call-done = f32[256,256]{1,0:T(8,128)} async-done(((f32[256,256]{1,0:T(8,128)}), f32[256,256]{1,0:T(8,128)}) %all-reduce.9.cloned.1.call-update) | async-done | bytes 262160 | tf_op jit(solution)/shard_map/psum | solution.py:53
  547.3 1.2 fusion.1
  548.5 1.1 fusion.20
  549.6 0.0 all-reduce.11.cloned.1.call-update
  549.7 0.0 all-to-all-done.1
  549.7 0.2 multiply_bitcast_fusion
  549.9 1.5 copy.40
  551.4 2.0 mul.101
  553.5 4.0 sub.15
  557.5 101.2 %all-reduce.11.cloned.1.call-done = f32[256,256]{1,0:T(8,128)} async-done(((f32[256,256]{1,0:T(8,128)}), f32[256,256]{1,0:T(8,128)}) %all-reduce.11.cloned.1.call-update) | async-done | bytes 262160 | tf_op jit(solution)/shard_map/psum | solution.py:53
  658.7 1.8 fusion
Async XLA Ops:
  8.0 29.7 %all-reduce.5.cloned.1.call-start = ((), (), s32[]{:S(2)}) async-start(), calls=%async_computation.3 | async-start | bytes 5242880 | tf_op jit(solution)/shard_map/psum | solution.py:33
  12.6 115.6 %copy-start.1 = (f32[576,256]{1,0:T(8,128)S(1)}, f32[576,256]{1,0:T(8,128)}, u32[]{:S(2)}) copy-start(f32[576,256]{1,0:T(8,128)} %param.13) | copy-start | bytes 1769476
  37.7 90.4 %all-to-all-start = ((f32[64,16,576]{2,0,1:T(8,128)}), f32[64,16,576]{2,0,1:T(8,128)S(1)}, u32[]{:S(2)}, u32[]{:S(2)}) async-start(f32[64,16,576]{2,0,1:T(8,128)} %all-reduce.5.cloned.1.call-done), calls=%async_computation | async-start | bytes 5242880 | tf_op jit(solution)/shard_map/all_to_all | solution.py:34
  44.5 83.6 %all-gather.4.cloned.1.call-start = ((), (), s32[]{:S(2)}) async-start(), calls=%async_computation.4 | async-start | bytes 1114112 | tf_op jit(solution)/shard_map/all_gather | solution.py:35
  45.1 175.7 %reduce-scatter.4.cloned.1.call-start = ((), (), s32[]{:S(2)}) async-start(), calls=%async_computation.9 | async-start | bytes 1114112
  140.4 82.5 %copy-start = (f32[1024,256]{1,0:T(8,128)S(1)}, f32[1024,256]{1,0:T(8,128)}, u32[]{:S(2)}) copy-start(f32[1024,256]{1,0:T(8,128)} %all-gather.4.cloned.1.call-done) | copy-start | bytes 3145732
  143.0 180.3 %all-gather.6.cloned.1.call-start = ((), (), s32[]{:S(2)}) async-start(), calls=%async_computation.8 | async-start | bytes 4456448 | tf_op jit(solution)/shard_map/all_gather | solution.py:46
  228.6 321.1 %all-to-all-start.1 = ((f32[16,64,576]{2,1,0:T(8,128)}), f32[16,64,576]{2,1,0:T(8,128)S(1)}, u32[]{:S(2)}, u32[]{:S(2)}) async-start(f32[16,64,576]{2,1,0:T(8,128)} %bitcast.31), calls=%async_computation.1 | async-start | bytes 5242880 | tf_op jit(solution)/shard_map/all_to_all | solution.py:44
  232.3 94.9 %copy-start.2 = (f32[64,256]{1,0:T(8,128)S(1)}, f32[64,256]{1,0:T(8,128)}, u32[]{:S(2)}) copy-start(f32[64,256]{1,0:T(8,128)} %reduce-scatter.4.cloned.1.call-done) | copy-start | bytes 196612
  232.3 203.0 %all-reduce.7.cloned.1.call-start = ((), (), s32[]{:S(2)}) async-start(), calls=%async_computation.5 | async-start | bytes 524288 | tf_op jit(solution)/shard_map/psum | solution.py:49
  323.3 114.4 %copy-start.6 = (f32[1,2,64]{2,1,0:T(2,128)S(1)}, f32[1,2,64]{2,1,0:T(2,128)}, u32[]{:S(2)}) copy-start(f32[1,2,64]{2,1,0:T(2,128)} %param.10) | copy-start | bytes 1540
  323.3 116.9 %copy-start.3 = (f32[2,64]{1,0:T(2,128)S(1)}, f32[2,64]{1,0:T(2,128)}, u32[]{:S(2)}) copy-start(f32[2,64]{1,0:T(2,128)} %param.15) | copy-start | bytes 1540
  323.3 116.9 %copy-start.4 = (f32[2,64]{1,0:T(2,128)S(1)}, f32[2,64]{1,0:T(2,128)}, u32[]{:S(2)}) copy-start(f32[2,64]{1,0:T(2,128)} %param.16) | copy-start | bytes 1540
  323.3 116.9 %copy-start.5 = (f32[2,64]{1,0:T(2,128)S(1)}, f32[2,64]{1,0:T(2,128)}, u32[]{:S(2)}) copy-start(f32[2,64]{1,0:T(2,128)} %param.17) | copy-start | bytes 1540
  328.4 218.9 %all-reduce.9.cloned.1.call-start = ((), (), s32[]{:S(2)}) async-start(), calls=%async_computation.6 | async-start | bytes 524288 | tf_op jit(solution)/shard_map/psum | solution.py:53
  437.7 221.0 %all-reduce.11.cloned.1.call-start = ((), (), s32[]{:S(2)}) async-start(), calls=%async_computation.7 | async-start | bytes 524288 | tf_op jit(solution)/shard_map/psum | solution.py:53
Sparse Core Ops, SparseCore 0:
  12.7 24.9 all-reduce.4
Sparse Core Ops, SparseCore 1:
  47.8 80.3 all-gather.3
  143.1 77.7 reduce-scatter.3
  224.0 99.2 all-gather.5
  329.1 106.1 all-reduce.6
  441.1 106.1 all-reduce.8
  552.5 106.1 all-reduce.10
